TPU v7x, 32 devices: a whole 2x2x4 slice. The times are simulated.
32 devices in a mesh: ep: 8 (over z, x), tp: 4 (over y, core).
Axes of the slice: x: 2, y: 2, z: 4, core: 2. Of those that a mesh axis runs over, the one named last changes fastest.
Arguments:
- hidden_in: bfloat16 [2048, 3584], P('ep', 'tp'), may hold values from -6 to 6
- moe_gain: bfloat16 [3584], replicated, may hold values from 0.099609375 to 1.8984375
- router_weight: bfloat16 [3584, 256], P('tp'), may hold values from -0.09375 to 0.09375
- expert_ids: int32 [2048, 8], P('ep'), may hold values from 0 to 255, all different within a row; in each aligned block of 256 rows (0 to 255, 256 to 511, ...) at most 16 rows name the same one
- shared_gate: bfloat16 [3584, 1024], P(None, 'tp'), may hold values from -0.09375 to 0.09375
- shared_up: bfloat16 [3584, 1024], P(None, 'tp'), may hold values from -0.09375 to 0.09375
- shared_down: bfloat16 [1024, 3584], P('tp'), may hold values from -0.1875 to 0.1875
- expert_gate: bfloat16 [8, 3584, 1024], P('ep', None, 'tp'), may hold values from -0.09375 to 0.09375
- expert_up: bfloat16 [8, 3584, 1024], P('ep', None, 'tp'), may hold values from -0.09375 to 0.09375
- expert_down: bfloat16 [8, 1024, 3584], P('ep', 'tp'), may hold values from -0.1875 to 0.1875
- attn_gain: bfloat16 [3584], P('tp'), may hold values from 0.099609375 to 1.8984375
- kv_down: bfloat16 [3584, 576], P('tp'), may hold values from -0.09375 to 0.09375
- kv_gain: bfloat16 [512], replicated, may hold values from 0.099609375 to 1.8984375
- doc_lengths: int32 [8, 4], P('ep'), may hold values from 1 to 128, 256 in all within a row
- page_table: int32 [8, 4], P('ep'), may hold values from 0 to 3, each once within a row
Outputs:
- layer_out: bfloat16 [2048, 3584], P('ep', 'tp')
- kv_pages: bfloat16 [8, 4, 64, 576], P('ep', 'tp')
Inputs may be any that keep to these rules, and one draw needn't show every extreme that they name: `expert_ids`: each row names 8 different experts. Among the rows of one ep index no expert is named more than 16 times. `doc_lengths`: each row sums to 256. `page_table`: each row holds every number below 4 once.
All inputs are finite; a program needn't handle non-finite values.
Results may differ from a plain program's by a relative error of at most 0.0065.
Values may be sent and summed in bfloat16 or wider, within the bound.
No kernel may reach another device: no remote copies, remote signals or barrier semaphores. Data moves between devices by JAX's collectives and lax.ppermute only.
A program may use at most 128 MiB of HBM per device.

v0:
```python
import jax
import jax.numpy as jnp
from jax import lax
from jax.sharding import PartitionSpec as P

CAP = 16
KVR = 512
EPS = 1e-06
ROUTE_SCALE = 2.5
THETA = 10000.0


def silu(values):
    return values / (1.0 + jnp.exp(-values))


def route_weights(logits, expert_ids):
    scores = 1.0 / (1.0 + jnp.exp(-logits))
    picked = jnp.take_along_axis(scores, expert_ids, axis=1)
    return ROUTE_SCALE * picked / jnp.sum(picked, axis=1, keepdims=True)


def slot_table(expert_ids, gate_weights, expert_count, capacity):
    token_count = expert_ids.shape[0]
    columns = jnp.arange(expert_count, dtype=jnp.int32)
    matched = expert_ids[:, :, None] == columns[None, None, :]
    weight_rows = jnp.sum(jnp.where(matched, gate_weights[:, :, None], 0.0), axis=1)
    chosen = jnp.any(matched, axis=1).astype(jnp.int32)
    before = jnp.cumsum(chosen, axis=0) - chosen
    target = jnp.where(chosen > 0, columns[None, :] * capacity + before, expert_count * capacity)
    token_index = jnp.broadcast_to(jnp.arange(token_count, dtype=jnp.int32)[:, None], target.shape)
    slot_token = (
        jnp.full((expert_count * capacity + 1,), token_count, jnp.int32)
        .at[target.reshape(-1)]
        .set(token_index.reshape(-1))
    )
    slot_weight = (
        jnp.zeros((expert_count * capacity + 1,), jnp.float32)
        .at[target.reshape(-1)]
        .set(weight_rows.reshape(-1))
    )
    return (slot_token[:-1], slot_weight[:-1])


def positions_of(lengths, token_count):
    doc_ends = jnp.cumsum(lengths)
    doc_starts = doc_ends - lengths
    token_index = jnp.arange(token_count, dtype=jnp.int32)
    doc_begin = jnp.max(
        jnp.where(doc_starts[None, :] <= token_index[:, None], doc_starts[None, :], 0), axis=1
    )
    return (token_index - doc_begin).astype(jnp.float32)


def rotate(rope_part, position):
    half_width = rope_part.shape[1] // 2
    frequency = THETA ** (-jnp.arange(half_width, dtype=jnp.float32) * 2.0 / rope_part.shape[1])
    angles = position[:, None] * frequency[None, :]
    cosine = jnp.cos(angles)
    sine_part = jnp.sin(angles)
    first_half = rope_part[:, :half_width]
    second_half = rope_part[:, half_width:]
    return jnp.concatenate(
        [
            first_half * cosine - second_half * sine_part,
            second_half * cosine + first_half * sine_part,
        ],
        axis=1,
    )


def finish(latent, position, kv_gain):
    plain_part = latent[:, :KVR]
    row_scale = lax.rsqrt(jnp.mean(plain_part * plain_part, axis=1, keepdims=True) + EPS)
    normed = plain_part * row_scale * kv_gain.astype(jnp.float32)
    return jnp.concatenate([normed, rotate(latent[:, KVR:], position)], axis=1).astype(jnp.bfloat16)


def per_device(
    hidden_in,
    moe_gain,
    router_weight,
    expert_ids,
    shared_gate,
    shared_up,
    shared_down,
    expert_gate,
    expert_up,
    expert_down,
    attn_gain,
    kv_down,
    kv_gain,
    doc_lengths,
    page_table,
):
    groups = lax.axis_size("ep")
    tp_count = lax.axis_size("tp")
    member = lax.axis_index("tp")
    tok_rows, width_local = hidden_in.shape
    full_width = width_local * tp_count
    capacity = CAP
    gathered = lax.all_gather(hidden_in, "tp", axis=1, tiled=True)
    stream = gathered.astype(jnp.float32)
    inverse = lax.rsqrt(jnp.mean(stream * stream, axis=1, keepdims=True) + EPS)
    normed = (stream * inverse * moe_gain.astype(jnp.float32)).astype(jnp.bfloat16)
    normed_local = lax.dynamic_slice_in_dim(normed, member * width_local, width_local, 1)
    logits = lax.psum(
        jnp.dot(normed_local, router_weight, preferred_element_type=jnp.float32).astype(
            jnp.bfloat16
        ),
        "tp",
    ).astype(jnp.float32)
    gate_weights = route_weights(logits, expert_ids)
    slot_token, slot_weight = slot_table(expert_ids, gate_weights, groups, capacity)
    shared_hidden = (
        silu(jnp.dot(normed, shared_gate, preferred_element_type=jnp.float32))
        * jnp.dot(normed, shared_up, preferred_element_type=jnp.float32)
    ).astype(jnp.bfloat16)
    shared_part = jnp.dot(shared_hidden, shared_down, preferred_element_type=jnp.float32)
    w_gate = expert_gate[0]
    w_up = expert_up[0]
    w_down = expert_down[0]
    padded = jnp.concatenate([normed, jnp.zeros((1, full_width), jnp.bfloat16)], axis=0)
    send_rows = padded[slot_token].reshape(groups, capacity, full_width)
    arrived_block = lax.all_to_all(send_rows, "ep", split_axis=0, concat_axis=0, tiled=True)
    flat_rows = arrived_block.reshape(-1, full_width)
    hidden_rows = (
        silu(jnp.dot(flat_rows, w_gate, preferred_element_type=jnp.float32))
        * jnp.dot(flat_rows, w_up, preferred_element_type=jnp.float32)
    ).astype(jnp.bfloat16)
    result = jnp.dot(hidden_rows, w_down, preferred_element_type=jnp.float32)
    outputs = result.reshape(arrived_block.shape[0], arrived_block.shape[1], full_width)
    reduced = lax.psum_scatter(outputs, "tp", scatter_dimension=2, tiled=True)
    returned = lax.all_to_all(reduced, "ep", split_axis=0, concat_axis=0, tiled=True)
    weighted = returned.reshape(groups * capacity, width_local) * slot_weight[:, None]
    routed = jax.ops.segment_sum(weighted, slot_token, num_segments=tok_rows + 1)[:tok_rows]
    branch_sum = lax.psum_scatter(shared_part, "tp", scatter_dimension=1, tiled=True) + routed
    layer_out = (hidden_in.astype(jnp.float32) + branch_sum).astype(jnp.bfloat16)
    out_values = layer_out.astype(jnp.float32)
    scaled = (out_values * attn_gain.astype(jnp.float32)).astype(jnp.bfloat16)
    latent_part = jnp.dot(scaled, kv_down, preferred_element_type=jnp.float32)
    squares = jnp.sum(out_values * out_values, axis=1)
    positions = positions_of(doc_lengths[0], tok_rows)
    page_count = page_table.shape[1]
    per_owner = page_count // tp_count
    page_len = tok_rows // page_count
    own_slots = lax.dynamic_slice_in_dim(page_table[0], member * per_owner, per_owner, 0)
    latent_sum, energy = lax.psum((latent_part, squares), "tp")
    latent = latent_sum * lax.rsqrt(energy / full_width + EPS)[:, None]
    row_index = (
        own_slots[:, None] * page_len + jnp.arange(page_len, dtype=jnp.int32)[None, :]
    ).reshape(-1)
    cache_rows = finish(latent[row_index], positions[row_index], kv_gain)
    page_out = cache_rows.reshape(1, per_owner, page_len, cache_rows.shape[-1])
    return (layer_out, page_out)


def solution(mesh):
    placed = (
        P("ep", "tp"),
        P(),
        P("tp", None),
        P("ep", None),
        P(None, "tp"),
        P(None, "tp"),
        P("tp", None),
        P("ep", None, "tp"),
        P("ep", None, "tp"),
        P("ep", "tp", None),
        P("tp"),
        P("tp", None),
        P(),
        P("ep", None),
        P("ep", None),
    )
    return jax.shard_map(
        per_device,
        mesh=mesh,
        in_specs=placed,
        out_specs=(P("ep", "tp"), P("ep", "tp", None, None)),
        check_vma=False,
    )
```

profile of v0, /device:TPU:0, one launch (start us, length us, event | category | flops | bytes accessed | tf_op | source)
XLA Modules:
  0.0 229.4 jit_solution(17543167574252839877)
XLA Ops:
  8.0 0.7 fusion.33
  10.7 8.0 %scatter_custom_fusion = s32[129]{0:T(256)S(1)} fusion(s32[2048]{0:T(1024)S(1)} %bitcast.59, s32[2048]{0:T(1024)S(1)} %reshape.239, s32[]{:T(128)} %constant.28.clone.1), kind=kCustom, calls=%fused_computation.93 | custom fusion | bytes 520 | tf_op jit(solution)/shard_map/scatter | solution.py:35
  18.8 14.7 %all-gather.2.cloned.1.call-done = bf16[256,3584]{1,0:T(8,128)(2,1)} async-done(((bf16[256,896]{1,0:T(8,128)(2,1)}), bf16[256,3584]{1,0:T(8,128)(2,1)}) %all-gather.2.cloned.1.call-update) | async-done | bytes 1835024 | tf_op jit(solution)/shard_map/all_gather | solution.py:102
  33.4 2.1 fusion
  36.1 1.2 copy-done.1
  37.3 1.4 concatenate.20
  38.7 3.8 %gather_fusion = bf16[128,3584]{1,0:T(8,128)(2,1)S(1)} fusion(bf16[257,3584]{1,0:T(8,128)(2,1)} %concatenate.20, s32[1024]{0:T(1024)S(1)} %pad_clamp_fusion.1), kind=kCustom, calls=%fused_computation | custom fusion | bytes 1835520 | tf_op jit(solution)/shard_map/gather | solution.py:124
  42.5 29.1 %all_to_all.10 = bf16[8,16,3584]{2,1,0:T(8,128)(2,1)S(1)} all-to-all(bf16[8,16,3584]{2,1,0:T(8,128)(2,1)S(1)} %bitcast.57), channel_id=1, replica_groups=mesh['ep'=8,'tp'=4] {'ep'}, dimensions={0} | all-to-all | bytes 1835008 | tf_op jit(solution)/shard_map/all_to_all | solution.py:125
  72.1 1.1 copy-done.6
  73.6 1.1 copy-done.3
  74.7 1.7 fusion.3
  76.4 0.9 copy-done.9
  77.4 2.0 convolution_convert_fusion
  79.4 2.8 %fusion.56 = f32[256,256]{1,0:T(8,128)S(1)} fusion(bf16[256,3584]{1,0:T(8,128)(2,1)} %copy-done.1, bf16[3584,256]{1,0:T(8,128)(2,1)} %param.19), kind=kOutput, calls=%fused_computation.97 | convolution fusion | flops 469762048 | bytes 3932160 | tf_op jit(solution)/shard_map/dot_general | solution.py:116
  82.2 6.1 %fusion.13 = f32[256,3584]{1,0:T(8,128)} fusion(bf16[256,3584]{1,0:T(8,128)(2,1)S(1)} %copy-done, bf16[256,3584]{1,0:T(8,128)(2,1)} %copy-done.1, bf16[3584,256]{1,0:T(8,128)(2,1)} %param.20, f32[256,256]{1,0:T(8,128)S(1)} %fusion.56), kind=kOutput, calls=%fused_computation.24 | convolution fusion | flops 939851776 | bytes 9437184 | tf_op jit(solution)/shard_map/dot_general | solution.py:119
  89.9 14.1 %reduce-scatter.5.cloned.1.call-done = f32[8,16,896]{2,1,0:T(8,128)} async-done(((f32[8,16,3584]{2,1,0:T(8,128)}), f32[8,16,896]{2,1,0:T(8,128)}) %reduce-scatter.5.cloned.1.call-update) | async-done | bytes 458768 | tf_op jit(solution)/shard_map/reduce_scatter | solution.py:133
  103.9 5.5 %all-to-all-start.1 = ((f32[8,16,896]{2,1,0:T(8,128)}), f32[8,16,896]{2,1,0:T(8,128)S(1)}, u32[]{:S(2)}, u32[]{:S(2)}) async-start(f32[8,16,896]{2,1,0:T(8,128)} %reduce-scatter.5.cloned.1.call-done), calls=%async_computation.3 | async-start | bytes 917504 | tf_op jit(solution)/shard_map/all_to_all | solution.py:134
  110.4 0.8 gather_fusion.2
  111.2 27.4 %all-reduce.4.cloned.1.call-done = bf16[256,256]{1,0:T(8,128)(2,1)} async-done(((bf16[256,256]{1,0:T(8,128)(2,1)}), bf16[256,256]{1,0:T(8,128)(2,1)}) %all-reduce.4.cloned.1.call-update) | async-done | bytes 131088 | tf_op jit(solution)/shard_map/psum | solution.py:107
  138.6 1.0 add_divide_fusion
  139.6 16.6 %gather_fusion.3 = f32[2048]{0:T(1024)S(1)} fusion(f32[256,256]{1,0:T(8,128)S(1)} %add_divide_fusion, s32[2048]{0:T(1024)S(1)} %reshape.229), kind=kCustom, calls=%fused_computation.3 | custom fusion | bytes 32768 | tf_op jit(solution)/shard_map/jit(take_along_axis)/gather | solution.py:19
  156.7 8.0 %scatter_custom_fusion.1 = f32[129]{0:T(256)S(1)} fusion(s32[2048]{0:T(1024)S(1)} %bitcast.60, f32[2048]{0:T(1024)S(1)} %reshape.247, f32[]{:T(128)} %constant.24.clone.1), kind=kCustom, calls=%fused_computation.88 | custom fusion | bytes 520 | tf_op jit(solution)/shard_map/scatter | solution.py:40
  164.8 0.9 bitcast_multiply_fusion
  165.7 2.3 %scatter_custom_fusion.2 = f32[257,896]{1,0:T(8,128)S(1)} fusion(s32[128]{0:T(128)S(1)} %get-tuple-element.7, f32[128,896]{1,0:T(8,128)} %bitcast_multiply_fusion, f32[]{:T(128)} %constant.24.clone.1), kind=kCustom, calls=%fused_computation.31 | custom fusion | flops 114688 | bytes 921600 | tf_op jit(solution)/shard_map/scatter-add | solution.py:136
  168.0 14.1 %reduce-scatter.3.cloned.1.call-done = f32[256,896]{1,0:T(8,128)} async-done(((f32[256,3584]{1,0:T(8,128)}), f32[256,896]{1,0:T(8,128)}) %reduce-scatter.3.cloned.1.call-update) | async-done | bytes 917520 | tf_op jit(solution)/shard_map/reduce_scatter | solution.py:137
  182.1 1.5 fusion.18
  183.7 0.8 copy-done.7
  184.4 1.3 fusion.23
  185.8 5.8 %psum.23 = f32[256]{0:T(256)S(1)} all-reduce(f32[256]{0:T(256)S(1)} %get-tuple-element.2), channel_id=1, replica_groups=mesh['ep'=8,'tp'=4] {'tp'}, use_global_device_ids=true, to_apply=%region_14.15 | all-reduce | flops 256 | bytes 2048 | tf_op jit(solution)/shard_map/psum | solution.py:148
  191.6 28.2 %all-reduce.6.cloned.1.call-done = f32[256,576]{0,1:T(8,128)} async-done(((f32[256,576]{0,1:T(8,128)}), f32[256,576]{0,1:T(8,128)}) %all-reduce.6.cloned.1.call-update) | async-done | bytes 589840 | tf_op jit(solution)/shard_map/psum | solution.py:148
  219.7 1.1 broadcast_multiply_fusion
  222.2 0.7 pad_maximum_fusion
  (83 shorter events, 8.5 us)
Async XLA Ops:
  7.2 75.1 %copy-start = (bf16[256,3584]{1,0:T(8,128)(2,1)S(1)}, bf16[256,3584]{1,0:T(8,128)(2,1)}, u32[]{:S(2)}) copy-start(bf16[256,3584]{1,0:T(8,128)(2,1)} %param.21) | copy-start | bytes 5505028
  7.2 26.3 %all-gather.2.cloned.1.call-start = ((), (), s32[]{:S(2)}) async-start(), calls=%async_computation.4 | async-start | bytes 2293760 | tf_op jit(solution)/shard_map/all_gather | solution.py:102
  7.9 96.0 %reduce-scatter.5.cloned.1.call-start = ((), (), s32[]{:S(2)}) async-start(), calls=%async_computation.6 | async-start | bytes 2293760 | tf_op jit(solution)/shard_map/reduce_scatter | solution.py:133
  33.4 2.1 copy-start.2
  36.1 1.3 copy-start.1
  42.5 29.1 %copy-start.5 = (bf16[1,3584,256]{2,1,0:T(8,128)(2,1)S(1)}, bf16[1,3584,256]{2,1,0:T(8,128)(2,1)}, u32[]{:S(2)}) copy-start(bf16[1,3584,256]{2,1,0:T(8,128)(2,1)} %param.22) | copy-start | bytes 5505028
  71.7 1.5 copy-start.6
  73.2 1.5 copy-start.3
  76.4 1.0 copy-start.9
  76.4 62.2 %all-reduce.4.cloned.1.call-start = ((), (), s32[]{:S(2)}) async-start(), calls=%async_computation.7 | async-start | bytes 262144 | tf_op jit(solution)/shard_map/psum | solution.py:107
  82.2 99.9 %reduce-scatter.3.cloned.1.call-start = ((), (), s32[]{:S(2)}) async-start(), calls=%async_computation.5 | async-start | bytes 4587520 | tf_op jit(solution)/shard_map/reduce_scatter | solution.py:137
  88.3 0.7 copy-start.14
  88.3 0.8 copy-start.13
  88.3 1.5 copy-start.10
  88.3 21.8 %copy-start.12 = (bf16[512]{0:T(512)(128)(2,1)S(1)}, bf16[512]{0:T(512)(128)(2,1)}, u32[]{:S(2)}) copy-start(bf16[512]{0:T(512)(128)(2,1)} %param.27) | copy-start | bytes 3076
  88.3 21.8 %copy-start.11 = (bf16[896]{0:T(1024)(128)(2,1)S(1)}, bf16[896]{0:T(1024)(128)(2,1)}, u32[]{:S(2)}) copy-start(bf16[896]{0:T(1024)(128)(2,1)} %param.25) | copy-start | bytes 5380
  103.9 60.9 %all-to-all-start.1 = ((f32[8,16,896]{2,1,0:T(8,128)}), f32[8,16,896]{2,1,0:T(8,128)S(1)}, u32[]{:S(2)}, u32[]{:S(2)}) async-start(f32[8,16,896]{2,1,0:T(8,128)} %reduce-scatter.5.cloned.1.call-done), calls=%async_computation.3 | async-start | bytes 917504 | tf_op jit(solution)/shard_map/all_to_all | solution.py:134
  109.4 110.3 %all-reduce.6.cloned.1.call-start = ((), (), s32[]{:S(2)}) async-start(), calls=%async_computation.8 | async-start | bytes 1179648 | tf_op jit(solution)/shard_map/psum | solution.py:148
  156.2 25.9 %copy-start.4 = (bf16[256,896]{1,0:T(8,128)(2,1)S(1)}, bf16[256,896]{1,0:T(8,128)(2,1)}, u32[]{:S(2)}) copy-start(bf16[256,896]{1,0:T(8,128)(2,1)} %param.15) | copy-start | bytes 1376260
  182.1 2.3 %copy-start.8 = (bf16[896,576]{0,1:T(8,128)(2,1)S(1)}, bf16[896,576]{0,1:T(8,128)(2,1)}, u32[]{:S(2)}) copy-start(bf16[896,576]{0,1:T(8,128)(2,1)} %param.26) | copy-start | bytes 3096580
  183.7 0.8 copy-start.7
Sparse Core Ops, SparseCore 0:
  9.6 23.8 all-gather.1
  76.5 27.3 reduce-scatter.4
  106.8 31.7 all-reduce.3
  141.0 41.0 reduce-scatter.2
  185.9 33.7 all-reduce.5
where the time goes:
time: 230 us; the launch traced here: 229 us
  waiting for transfers between devices  99.2 us (43%)
  local copies, waits for them, and re-layouts  46.6 us (20%)
  blocking collectives  34.9 us (15%)
  matrix products  14.7 us (6%)
  other arithmetic  14.3 us (6%)
  between operations  14.1 us (6%)
  starting transfers between devices  5.7 us (2%)
    all_to_all x1, blocking collectives, per_device(): lax.all_to_all(send_rows, 'ep', split_axis=0, concat_axis=0, tiled=True)  29.1 us
    psum x1, waiting for transfers between devices, per_device(): latent_sum, energy = lax.psum((latent_part, squares), 'tp')  28.2 us
    psum x1, waiting for transfers between devices, per_device(): lax.psum(jnp.dot(normed_local, router_weight, preferred_element_type=jnp....  27.4 us
    gather x5, local copies, waits for them, and re-layouts, route_weights(): picked = jnp.take_along_axis(scores, expert_ids, axis=1)  17 us
    all_gather x1, waiting for transfers between devices, per_device(): gathered = lax.all_gather(hidden_in, 'tp', axis=1, tiled=True)  14.7 us
    reduce_scatter x1, waiting for transfers between devices, per_device(): lax.psum_scatter(shared_part, 'tp', scatter_dimension=1, tiled=True)  14.1 us
    reduce_scatter x1, waiting for transfers between devices, per_device(): reduced = lax.psum_scatter(outputs, 'tp', scatter_dimension=2, tiled=True)  14.1 us
    scatter x1, local copies, waits for them, and re-layouts, slot_table(): slot_weight = jnp.zeros((expert_count * capacity + 1,), jnp.float32).at[t...  8.04 us
  transfers between devices with their start and end apart: 6, of which 5 were waited for; matrix products, arithmetic and copies ran while one was open for 23% of the time, Pallas kernels for 0%

commit v1 on v0

--- a/solution.py
+++ b/solution.py
@@ -1,3 +1,4 @@
+import functools
 import jax
 import jax.numpy as jnp
 from jax import lax
@@ -8,6 +9,14 @@
 EPS = 1e-06
 ROUTE_SCALE = 2.5
 THETA = 10000.0
+
+
+def face_refer(arr, bus_axis):
+    tmp = lax.all_gather(arr, axis_name=bus_axis).sum(axis=0)
+    return tmp
+
+
+attach_array = functools.partial(face_refer, bus_axis="tp")
 
 
 def silu(values):
@@ -104,11 +113,10 @@
     inverse = lax.rsqrt(jnp.mean(stream * stream, axis=1, keepdims=True) + EPS)
     normed = (stream * inverse * moe_gain.astype(jnp.float32)).astype(jnp.bfloat16)
     normed_local = lax.dynamic_slice_in_dim(normed, member * width_local, width_local, 1)
-    logits = lax.psum(
+    logits = attach_array(
         jnp.dot(normed_local, router_weight, preferred_element_type=jnp.float32).astype(
             jnp.bfloat16
-        ),
-        "tp",
+        )
     ).astype(jnp.float32)
     gate_weights = route_weights(logits, expert_ids)
     slot_token, slot_weight = slot_table(expert_ids, gate_weights, groups, capacity)

time: 230 us -> 196 us (0.85)
  waiting for transfers between devices: 99.2 us -> 59.5 us
  blocking collectives: 34.9 us -> 41.4 us
    psum x1 -> x0, waiting for transfers between devices: 27.4 us -> none  [per_device(): lax.psum(jnp.dot(normed_local, router_weight, preferred_element_type=jnp....]
    reduce_scatter x1, waiting for transfers between devices: 14.1 us -> 1.87 us  [per_device(): lax.psum_scatter(shared_part, 'tp', scatter_dimension=1, tiled=True)]
    all_gather x0 -> x1, blocking collectives: none -> 6.5 us  [face_refer(): tmp = lax.all_gather(arr, axis_name=bus_axis).sum(axis=0)]
  transfers between devices with their start and end apart: 6 -> 5, of which waited for: 5 -> 4; matrix products, arithmetic and copies ran while one was open for 23% -> 27% of each run, Pallas kernels for 0% -> 0%
where the time goes in v1:
time: 196 us; the launch traced here: 195 us
  waiting for transfers between devices  59.5 us (30%)
  local copies, waits for them, and re-layouts  45.8 us (23%)
  blocking collectives  41.4 us (21%)
  other arithmetic  14.5 us (7%)
  between operations  14.1 us (7%)
  matrix products  13.9 us (7%)
  starting transfers between devices  5.68 us (3%)
    all_to_all x1, blocking collectives, per_device(): lax.all_to_all(send_rows, 'ep', split_axis=0, concat_axis=0, tiled=True)  29.1 us
    psum x1, waiting for transfers between devices, per_device(): latent_sum, energy = lax.psum((latent_part, squares), 'tp')  28.2 us
    gather x5, local copies, waits for them, and re-layouts, route_weights(): picked = jnp.take_along_axis(scores, expert_ids, axis=1)  17 us
    all_gather x1, waiting for transfers between devices, per_device(): gathered = lax.all_gather(hidden_in, 'tp', axis=1, tiled=True)  14.7 us
    reduce_scatter x1, waiting for transfers between devices, per_device(): reduced = lax.psum_scatter(outputs, 'tp', scatter_dimension=2, tiled=True)  14.1 us
    scatter x1, local copies, waits for them, and re-layouts, slot_table(): slot_weight = jnp.zeros((expert_count * capacity + 1,), jnp.float32).at[t...  8.22 us
    scatter x1, local copies, waits for them, and re-layouts, slot_table(): slot_token = jnp.full((expert_count * capacity + 1,), token_count, jnp.in...  8.04 us
    all_gather x1, blocking collectives, face_refer(): tmp = lax.all_gather(arr, axis_name=bus_axis).sum(axis=0)  6.5 us
  transfers between devices with their start and end apart: 5, of which 4 were waited for; matrix products, arithmetic and copies ran while one was open for 27% of the time, Pallas kernels for 0%

profile of v1, /device:TPU:0, one launch (start us, length us, event | category | flops | bytes accessed | tf_op | source)
XLA Modules:
  0.0 194.9 jit_solution(14917667111120966947)
XLA Ops:
  8.0 0.7 fusion.33
  9.5 0.7 convert_element_type.61
  10.7 8.0 %scatter_custom_fusion = s32[129]{0:T(256)S(1)} fusion(s32[2048]{0:T(1024)S(1)} %bitcast.61, s32[2048]{0:T(1024)S(1)} %reshape.239, s32[]{:T(128)} %constant.28.clone.1), kind=kCustom, calls=%fused_computation.93 | custom fusion | bytes 520 | tf_op jit(solution)/shard_map/scatter | solution.py:44
  18.8 14.7 %all-gather.3.cloned.1.call-done = bf16[256,3584]{1,0:T(8,128)(2,1)} async-done(((bf16[256,896]{1,0:T(8,128)(2,1)}), bf16[256,3584]{1,0:T(8,128)(2,1)}) %all-gather.3.cloned.1.call-update) | async-done | bytes 1835024 | tf_op jit(solution)/shard_map/all_gather | solution.py:111
  33.4 2.1 %fusion = f32[256]{0:T(256)S(1)} fusion(bf16[256,3584]{1,0:T(8,128)(2,1)} %all-gather.3.cloned.1.call-done), kind=kLoop, calls=%fused_computation.9 | loop fusion | flops 2752256 | bytes 1836032 | tf_op jit(solution)/shard_map/reduce_sum | solution.py:113
  36.1 1.2 copy-done.1
  37.3 1.4 concatenate.20
  38.7 3.8 %gather_fusion = bf16[128,3584]{1,0:T(8,128)(2,1)S(1)} fusion(bf16[257,3584]{1,0:T(8,128)(2,1)} %concatenate.20, s32[1024]{0:T(1024)S(1)} %pad_clamp_fusion.1), kind=kCustom, calls=%fused_computation | custom fusion | bytes 1835520 | tf_op jit(solution)/shard_map/gather | solution.py:132
  42.5 29.1 %all_to_all.10 = bf16[8,16,3584]{2,1,0:T(8,128)(2,1)S(1)} all-to-all(bf16[8,16,3584]{2,1,0:T(8,128)(2,1)S(1)} %bitcast.58), channel_id=1, replica_groups=mesh['ep'=8,'tp'=4] {'ep'}, dimensions={0} | all-to-all | bytes 1835008 | tf_op jit(solution)/shard_map/all_to_all | solution.py:133
  72.1 1.1 copy-done.6
  73.6 1.1 copy-done.3
  74.7 1.7 fusion.3
  76.4 2.7 %fusion.56 = f32[256,256]{1,0:T(8,128)S(1)} fusion(bf16[256,3584]{1,0:T(8,128)(2,1)} %copy-done.1, bf16[3584,256]{1,0:T(8,128)(2,1)} %param.19), kind=kOutput, calls=%fused_computation.97 | convolution fusion | flops 469762048 | bytes 3932160 | tf_op jit(solution)/shard_map/dot_general | solution.py:124
  79.1 6.0 %fusion.13 = f32[256,3584]{1,0:T(8,128)} fusion(bf16[256,3584]{1,0:T(8,128)(2,1)S(1)} %copy-done, bf16[256,3584]{1,0:T(8,128)(2,1)} %copy-done.1, bf16[3584,256]{1,0:T(8,128)(2,1)} %param.20, f32[256,256]{1,0:T(8,128)S(1)} %fusion.56), kind=kOutput, calls=%fused_computation.24 | convolution fusion | flops 939851776 | bytes 9437184 | tf_op jit(solution)/shard_map/dot_general | solution.py:127
  87.7 0.8 gather_fusion.2
  88.5 1.3 convolution_convert_fusion
  89.8 14.1 %reduce-scatter.5.cloned.1.call-done = f32[8,16,896]{2,1,0:T(8,128)} async-done(((f32[8,16,3584]{2,1,0:T(8,128)}), f32[8,16,896]{2,1,0:T(8,128)}) %reduce-scatter.5.cloned.1.call-update) | async-done | bytes 458768 | tf_op jit(solution)/shard_map/reduce_scatter | solution.py:141
  103.9 5.5 %all-to-all-start.1 = ((f32[8,16,896]{2,1,0:T(8,128)}), f32[8,16,896]{2,1,0:T(8,128)}, u32[]{:S(2)}, u32[]{:S(2)}) async-start(f32[8,16,896]{2,1,0:T(8,128)} %reduce-scatter.5.cloned.1.call-done), calls=%async_computation.3 | async-start | bytes 917504 | tf_op jit(solution)/shard_map/all_to_all | solution.py:142
  109.4 6.5 %all-gather = bf16[1024,256]{1,0:T(8,128)(2,1)S(1)} all-gather(bf16[256,256]{1,0:T(8,128)(2,1)S(1)} %convolution_convert_fusion), channel_id=2, replica_groups=mesh['ep'=8,'tp'=4] {'tp'}, dimensions={0}, use_global_device_ids=true | all-gather | bytes 655360 | tf_op jit(solution)/shard_map/all_gather | solution.py:15
  116.1 16.6 %gather_fusion.3 = f32[2048]{0:T(1024)S(1)} fusion(f32[256,256]{1,0:T(8,128)S(1)} %add_divide_fusion, s32[2048]{0:T(1024)S(1)} %reshape.229), kind=kCustom, calls=%fused_computation.3 | custom fusion | bytes 32768 | tf_op jit(solution)/shard_map/jit(take_along_axis)/gather | solution.py:28
  133.3 8.2 %scatter_custom_fusion.1 = f32[129]{0:T(256)S(1)} fusion(s32[2048]{0:T(1024)S(1)} %bitcast.62, f32[2048]{0:T(1024)S(1)} %reshape.247, f32[]{:T(128)} %constant.24.clone.1), kind=kCustom, calls=%fused_computation.88 | custom fusion | bytes 520 | tf_op jit(solution)/shard_map/scatter | solution.py:49
  141.5 1.9 bitcast_multiply_fusion
  143.4 2.3 %scatter_custom_fusion.2 = f32[257,896]{1,0:T(8,128)S(1)} fusion(s32[128]{0:T(128)S(1)} %get-tuple-element.7, f32[128,896]{1,0:T(8,128)} %bitcast_multiply_fusion, f32[]{:T(128)} %constant.24.clone.1), kind=kCustom, calls=%fused_computation.31 | custom fusion | flops 114688 | bytes 921600 | tf_op jit(solution)/shard_map/scatter-add | solution.py:144
  145.7 1.9 reduce-scatter.3.cloned.1.call-done
  147.6 1.5 fusion.18
  149.1 0.8 copy-done.7
  149.9 1.3 fusion.23
  151.3 5.8 %psum.15 = f32[256]{0:T(256)S(1)} all-reduce(f32[256]{0:T(256)S(1)} %get-tuple-element.2), channel_id=1, replica_groups=mesh['ep'=8,'tp'=4] {'tp'}, use_global_device_ids=true, to_apply=%region_14.15 | all-reduce | flops 256 | bytes 2048 | tf_op jit(solution)/shard_map/psum | solution.py:156
  157.0 28.2 %all-reduce.3.cloned.1.call-done = f32[256,576]{0,1:T(8,128)} async-done(((f32[256,576]{0,1:T(8,128)}), f32[256,576]{0,1:T(8,128)}) %all-reduce.3.cloned.1.call-update) | async-done | bytes 589840 | tf_op jit(solution)/shard_map/psum | solution.py:156
  185.2 1.1 broadcast_multiply_fusion
  186.6 0.7 gather_fusion.1
  187.7 0.7 pad_maximum_fusion
  (82 shorter events, 7.2 us)
Async XLA Ops:
  7.2 72.0 %copy-start = (bf16[256,3584]{1,0:T(8,128)(2,1)S(1)}, bf16[256,3584]{1,0:T(8,128)(2,1)}, u32[]{:S(2)}) copy-start(bf16[256,3584]{1,0:T(8,128)(2,1)} %param.21) | copy-start | bytes 5505028
  7.2 26.3 %all-gather.3.cloned.1.call-start = ((), (), s32[]{:S(2)}) async-start(), calls=%async_computation.4 | async-start | bytes 2293760 | tf_op jit(solution)/shard_map/all_gather | solution.py:111
  7.9 96.0 %reduce-scatter.5.cloned.1.call-start = ((), (), s32[]{:S(2)}) async-start(), calls=%async_computation.6 | async-start | bytes 2293760 | tf_op jit(solution)/shard_map/reduce_scatter | solution.py:141
  33.4 2.1 %copy-start.2 = (bf16[256,3584]{1,0:T(8,128)(2,1)S(1)}, bf16[256,3584]{1,0:T(8,128)(2,1)}, u32[]{:S(2)}) copy-start(bf16[256,3584]{1,0:T(8,128)(2,1)} %all-gather.3.cloned.1.call-done) | copy-start | bytes 5505028
  36.1 1.3 copy-start.1
  42.5 29.1 %copy-start.5 = (bf16[1,3584,256]{2,1,0:T(8,128)(2,1)S(1)}, bf16[1,3584,256]{2,1,0:T(8,128)(2,1)}, u32[]{:S(2)}) copy-start(bf16[1,3584,256]{2,1,0:T(8,128)(2,1)} %param.22) | copy-start | bytes 5505028
  71.7 1.5 copy-start.6
  73.2 1.5 copy-start.3
  76.4 71.2 %reduce-scatter.3.cloned.1.call-start = ((), (), s32[]{:S(2)}) async-start(), calls=%async_computation.5 | async-start | bytes 4587520 | tf_op jit(solution)/shard_map/reduce_scatter | solution.py:145
  85.2 0.7 copy-start.14
  85.2 0.8 copy-start.12
  85.2 0.8 copy-start.11
  85.2 0.8 copy-start.10
  85.2 1.1 copy-start.13
  85.2 3.3 %copy-start.9 = (bf16[896,256]{1,0:T(8,128)(2,1)S(1)}, bf16[896,256]{1,0:T(8,128)(2,1)}, u32[]{:S(2)}) copy-start(bf16[896,256]{1,0:T(8,128)(2,1)} %param.17) | copy-start | bytes 1376260
  103.9 37.6 %all-to-all-start.1 = ((f32[8,16,896]{2,1,0:T(8,128)}), f32[8,16,896]{2,1,0:T(8,128)}, u32[]{:S(2)}, u32[]{:S(2)}) async-start(f32[8,16,896]{2,1,0:T(8,128)} %reduce-scatter.5.cloned.1.call-done), calls=%async_computation.3 | async-start | bytes 917504 | tf_op jit(solution)/shard_map/all_to_all | solution.py:142
  109.4 75.8 %all-reduce.3.cloned.1.call-start = ((), (), s32[]{:S(2)}) async-start(), calls=%async_computation.7 | async-start | bytes 1179648 | tf_op jit(solution)/shard_map/psum | solution.py:156
  132.8 14.8 %copy-start.4 = (bf16[256,896]{1,0:T(8,128)(2,1)S(1)}, bf16[256,896]{1,0:T(8,128)(2,1)}, u32[]{:S(2)}) copy-start(bf16[256,896]{1,0:T(8,128)(2,1)} %param.15) | copy-start | bytes 1376260
  147.6 2.3 %copy-start.8 = (bf16[896,576]{0,1:T(8,128)(2,1)S(1)}, bf16[896,576]{0,1:T(8,128)(2,1)}, u32[]{:S(2)}) copy-start(bf16[896,576]{0,1:T(8,128)(2,1)} %param.26) | copy-start | bytes 3096580
  149.1 0.8 copy-start.7
Sparse Core Ops, SparseCore 0:
  9.6 23.8 all-gather.2
  76.5 27.3 reduce-scatter.4
  106.4 41.1 reduce-scatter.2
  151.4 33.8 all-reduce.2
